TPU v7x, 32 devices: a whole 2x2x4 slice. The times are simulated.
32 devices in a mesh: pairs: 2 (over x), src: 8 (over z, y), tgt: 2 (over core).
Axes of the slice: x: 2, y: 2, z: 4, core: 2. Of those that a mesh axis runs over, the one named last changes fastest.
Arguments:
- src_feat: float32 [2048, 32], P(('pairs', 'src'), 'tgt'), parts along dimension 0, may hold values from -0.72 to 0.72
- tgt_feat: float32 [32768, 32], P(('pairs', 'tgt'), 'src'), parts along dimension 0, may hold values from -0.72 to 0.72
- tgt_dual: float32 [32768], P(('pairs', 'tgt')), parts along dimension 0, may hold values from -6 to 6
- core_matrix: float32 [68, 34], P('pairs'), parts along dimension 0, may hold values from -3 to 3
Outputs:
- src_dual: float32 [2048], P(('pairs', 'src')), parts along dimension 0
- tgt_dual_out: float32 [32768], P(('pairs', 'tgt')), parts along dimension 0
- core_out: float32 [68, 34], P('pairs'), parts along dimension 0
There are 2 independent parts, one for each index of `pairs`. A program takes and returns all parts, laid end to end along the dimension named above; each array names one. Nothing has to cross between parts.
All inputs are finite; a program needn't handle non-finite values.
Results may differ from a plain program's by a relative error of at most 0.0003.
Values sent between devices are 32-bit elements; how exact they have to be, the bound alone decides.
No kernel may reach another device: no remote copies, remote signals or barrier semaphores. Data moves between devices by JAX's collectives and lax.ppermute only.
A program may use at most 64 MiB of HBM per device.

v0:
```python
import jax
import jax.numpy as jnp
from jax import lax
from jax.sharding import PartitionSpec as P

OUTER = 2
EPSILON = 0.02
HIGH = lax.Precision.HIGHEST


def merged(array, axis, combine):
    everything = jax.tree.map(lambda part: lax.all_gather(part, axis), array)
    leading = jax.tree.map(lambda part: part[0], everything)

    def step(k, so_far):
        return combine(so_far, jax.tree.map(lambda part: part[k], everything))

    return lax.fori_loop(1, lax.axis_size(axis), step, leading)


def lifted(values):
    squares = jnp.sum(values * values, axis=1, keepdims=True)
    ones = jnp.ones_like(squares)
    left = jnp.concatenate([squares, ones, -2.0 * values], axis=1)
    right = jnp.concatenate([ones, squares, values], axis=1)
    return (left, right)


def merge_logsum(earlier, later):
    top = jnp.maximum(earlier[0], later[0])
    return (top, earlier[1] * jnp.exp(earlier[0] - top) + later[1] * jnp.exp(later[0] - top))


def shards(src_feat, tgt_feat, tgt_dual, core_matrix):
    src_rows = lax.all_gather(src_feat, "tgt", axis=1, tiled=True)
    tgt_rows = lax.all_gather(tgt_feat, "src", axis=1, tiled=True)
    src_left, src_right = lifted(src_rows)
    tgt_left, tgt_right = lifted(tgt_rows)
    src_count = lax.axis_size("src")
    tgt_count = lax.axis_size("tgt")
    row_count = src_rows.shape[0]
    col_count = tgt_rows.shape[0]
    log_src = -jnp.log(jnp.float32(row_count * src_count))
    log_tgt = -jnp.log(jnp.float32(col_count * tgt_count))
    src_dual = jnp.zeros((row_count,), jnp.float32)
    for outer_step in range(OUTER):
        projected = jnp.dot(src_left, core_matrix, precision=HIGH)
        linear = jnp.dot(projected, tgt_right.T, precision=HIGH)
        row_logits = (tgt_dual[None, :] - linear) / EPSILON
        row_max = jnp.max(row_logits, axis=1)
        row_total = jnp.sum(jnp.exp(row_logits - row_max[:, None]), axis=1)
        row_max, row_total = merged((row_max, row_total), "tgt", merge_logsum)
        src_dual = EPSILON * log_src - EPSILON * (row_max + jnp.log(row_total))
        col_logits = (src_dual[:, None] - linear) / EPSILON
        col_max = jnp.max(col_logits, axis=0)
        col_exp = jnp.exp(col_logits - col_max[None, :])
        col_total = jnp.sum(col_exp, axis=0)
        piece_max, piece_total = (
            lax.all_to_all(col_max[None, :], "src", split_axis=1, concat_axis=0, tiled=True),
            lax.all_to_all(col_total[None, :], "src", split_axis=1, concat_axis=0, tiled=True),
        )
        whole_max = jnp.max(piece_max, axis=0)
        whole_total = jnp.sum(piece_total * jnp.exp(piece_max - whole_max[None, :]), axis=0)
        dual_piece = EPSILON * log_tgt - EPSILON * (whole_max + jnp.log(whole_total))
        tgt_dual = lax.all_gather(dual_piece, "src", axis=0, tiled=True)
        coupling = jnp.exp((src_dual[:, None] + tgt_dual[None, :] - linear) / EPSILON)
        weighted = jnp.dot(coupling, tgt_left, precision=HIGH)
        core_part = jnp.dot(src_right.T, weighted, precision=HIGH)
        core_matrix = -2.0 * lax.psum(core_part, ("src", "tgt"))
    return (src_dual, tgt_dual, core_matrix)


def solution(mesh):
    placed = (
        P(("pairs", "src"), "tgt"),
        P(("pairs", "tgt"), "src"),
        P(("pairs", "tgt")),
        P("pairs", None),
    )
    return jax.shard_map(
        shards,
        mesh=mesh,
        in_specs=placed,
        out_specs=(P(("pairs", "src")), P(("pairs", "tgt")), P("pairs", None)),
        check_vma=False,
    )
```

profile of v0, /device:TPU:0, one launch (start us, length us, event | category | flops | bytes accessed | tf_op | source)
XLA Modules:
  0.0 312.0 jit_solution(1951934580604606527)
XLA Ops:
  7.2 0.0 copy-start
  7.2 0.0 copy-start.3
  7.2 0.0 all-gather.11.cloned.1.call-start
  7.2 0.7 all-gather.11.cloned.1.call-update
  7.9 2.2 all_gather.36
  10.1 0.0 copy-done
  10.1 0.3 fusion.32
  10.4 42.7 %all-gather.11.cloned.1.call-done = f32[8,4,8192]{2,1,0:T(4,128)} async-done(((f32[1,4,8192]{2,1,0:T(4,128)}), f32[8,4,8192]{2,1,0:T(4,128)}) %all-gather.11.cloned.1.call-update) | async-done | bytes 1048592 | tf_op jit(solution)/shard_map/all_gather | solution.py:36
  53.2 1.6 reshape.132
  54.8 0.2 broadcast_multiply_fusion
  55.0 0.0 copy-done.3
  55.0 3.8 %fusion.10 = (f32[128]{0:T(128)S(1)}, f32[128,8192]{1,0:T(8,128)S(1)}) fusion(f32[8192]{0:T(1024)S(1)} %copy-done.3, f32[128,34]{1,0:T(8,128)S(1)} %fusion.32, f32[8192,32]{0,1:T(8,128)S(1)} %bitcast.89, f32[8192,1]{0,1:T(1,128)S(1)} %bitcast.91, f32[8192,1]{0,1:T(1,128)S(1)} %broadcast_in_dim.10), kind=kOutput, calls=%fused_computation.18 | convolution fusion | flops 431521664 | bytes 5359104 | tf_op jit(solution)/shard_map/dot_general | solution.py:48
  58.8 0.0 copy-start.2
  58.8 1.0 exponential_reduce_fusion.3
  59.8 1.8 all-gather.6
  61.6 1.8 all-gather.5
  63.4 1.2 fusion.11
  64.5 0.0 copy-done.2
  64.5 3.3 %all-to-all-start = ((f32[1,8,1024]{2,0,1:T(1,128)}), f32[1,8,1024]{2,0,1:T(1,128)S(1)}, u32[]{:S(2)}, u32[]{:S(2)}) async-start(f32[1,8,1024]{2,0,1:T(1,128)} %bitcast.11), calls=%async_computation | async-start | bytes 65536 | tf_op jit(solution)/shard_map/all_to_all | solution.py:59
  67.9 3.7 %exponential_reduce_fusion.2 = f32[8192]{0:T(1024)} fusion(f32[128,8192]{1,0:T(8,128)} %copy-done.2, f32[8192]{0:T(1024)} %fusion.11, f32[128]{0:T(128)S(1)} %multiply_subtract_fusion.3), kind=kLoop, calls=%fused_computation.14 | loop fusion | flops 4186112 | bytes 4260352 | tf_op jit(solution)/shard_map/reduce_sum | solution.py:57
  71.6 2.9 all-to-all-done
  74.6 3.3 %all-to-all-start.1 = ((f32[1,8,1024]{2,0,1:T(1,128)}), f32[1,8,1024]{2,0,1:T(1,128)S(1)}, u32[]{:S(2)}, u32[]{:S(2)}) async-start(f32[1,8,1024]{2,0,1:T(1,128)} %bitcast.12), calls=%async_computation.1 | async-start | bytes 65536 | tf_op jit(solution)/shard_map/all_to_all | solution.py:60
  77.9 6.6 %all-to-all-done.1 = f32[1,8,1024]{2,0,1:T(1,128)S(1)} async-done(((f32[1,8,1024]{2,0,1:T(1,128)}), f32[1,8,1024]{2,0,1:T(1,128)S(1)}, u32[]{:S(2)}, u32[]{:S(2)}) %all-to-all-start.1) | async-done | bytes 32800 | tf_op jit(solution)/shard_map/all_to_all | solution.py:60
  84.6 30.6 %all_gather.42 = f32[8192]{0:T(1024)S(1)} all-gather(f32[1024]{0:T(1024)S(1)} %multiply_subtract_fusion.1), channel_id=1, replica_groups=mesh['pairs'=2,'src'=8,'tgt'=2] {'src'}, dimensions={0}, use_global_device_ids=true | all-gather | bytes 36864 | tf_op jit(solution)/shard_map/all_gather | solution.py:65
  115.2 6.2 %fusion.5 = f32[128,34]{1,0:T(8,128)S(1)} fusion(f32[128,8192]{1,0:T(8,128)} %copy-done.2, f32[8192]{0:T(1024)S(1)} %all_gather.42, f32[128]{0:T(128)S(1)} %multiply_subtract_fusion.3, f32[8192,32]{0,1:T(8,128)S(1)} %get-tuple-element.27, f32[8192,1]{0,1:T(1,128)S(1)} %broadcast_in_dim.10, f32[8192,1]{0,1:T(1,128)S(1)} %bitcast.92), kind=kOutput, calls=%fused_computation.9 | convolution fusion | flops 431521792 | bytes 5359104 | tf_op jit(solution)/shard_map/dot_general | solution.py:67
  121.4 0.2 fusion.31
  121.6 57.8 %psum.14 = f32[34,34]{1,0:T(8,128)S(1)} all-reduce(f32[34,34]{1,0:T(8,128)S(1)} %fusion.31), channel_id=1, replica_groups=mesh['pairs'=2,'src'=8,'tgt'=2] {'src','tgt'}, use_global_device_ids=true, to_apply=%region_8.0 | all-reduce | flops 1156 | bytes 9248 | tf_op jit(solution)/shard_map/psum | solution.py:69
  179.4 0.3 fusion.28
  179.7 3.8 %fusion.12 = (f32[128]{0:T(128)S(1)}, f32[128,8192]{1,0:T(8,128)S(1)}) fusion(f32[8192]{0:T(1024)S(1)} %all_gather.42, f32[128,34]{1,0:T(8,128)S(1)} %fusion.28, f32[8192,32]{0,1:T(8,128)S(1)} %bitcast.90, f32[8192,1]{0,1:T(1,128)S(1)} %bitcast.93, f32[8192,1]{0,1:T(1,128)S(1)} %broadcast_in_dim.10), kind=kOutput, calls=%fused_computation.20 | convolution fusion | flops 431521664 | bytes 5359104 | tf_op jit(solution)/shard_map/dot_general | solution.py:48
  183.5 0.0 copy-start.1
  183.5 1.0 exponential_reduce_fusion.1
  184.5 1.8 all-gather.8
  186.3 1.8 all-gather.7
  188.1 0.0 copy-start.4
  188.1 1.1 fusion.13
  189.3 0.0 copy-done.1
  189.3 3.3 %all-to-all-start.2 = ((f32[1,8,1024]{2,0,1:T(1,128)}), f32[1,8,1024]{2,0,1:T(1,128)S(1)}, u32[]{:S(2)}, u32[]{:S(2)}) async-start(f32[1,8,1024]{2,0,1:T(1,128)} %bitcast.19), calls=%async_computation.2 | async-start | bytes 65536 | tf_op jit(solution)/shard_map/all_to_all | solution.py:59
  192.6 3.7 %exponential_reduce_fusion = f32[8192]{0:T(1024)} fusion(f32[128,8192]{1,0:T(8,128)} %copy-done.1, f32[8192]{0:T(1024)} %fusion.13, f32[128]{0:T(128)S(1)} %multiply_subtract_fusion.2), kind=kLoop, calls=%fused_computation.5 | loop fusion | flops 4186112 | bytes 4260352 | tf_op jit(solution)/shard_map/reduce_sum | solution.py:57
  196.4 2.9 all-to-all-done.2
  199.3 3.3 %all-to-all-start.3 = ((f32[1,8,1024]{2,0,1:T(1,128)}), f32[1,8,1024]{2,0,1:T(1,128)S(1)}, u32[]{:S(2)}, u32[]{:S(2)}) async-start(f32[1,8,1024]{2,0,1:T(1,128)} %bitcast.20), calls=%async_computation.3 | async-start | bytes 65536 | tf_op jit(solution)/shard_map/all_to_all | solution.py:60
  202.7 6.6 %all-to-all-done.3 = f32[1,8,1024]{2,0,1:T(1,128)S(1)} async-done(((f32[1,8,1024]{2,0,1:T(1,128)}), f32[1,8,1024]{2,0,1:T(1,128)S(1)}, u32[]{:S(2)}, u32[]{:S(2)}) %all-to-all-start.3) | async-done | bytes 32800 | tf_op jit(solution)/shard_map/all_to_all | solution.py:60
  209.3 30.6 %all_gather.47 = f32[8192]{0:T(1024)S(1)} all-gather(f32[1024]{0:T(1024)S(1)} %multiply_subtract_fusion), channel_id=1, replica_groups=mesh['pairs'=2,'src'=8,'tgt'=2] {'src'}, dimensions={0}, use_global_device_ids=true | all-gather | bytes 36864 | tf_op jit(solution)/shard_map/all_gather | solution.py:65
  239.9 0.0 copy-done.4
  239.9 6.2 %fusion = f32[128,34]{1,0:T(8,128)S(1)} fusion(f32[128,8192]{1,0:T(8,128)} %copy-done.1, f32[8192]{0:T(1024)S(1)} %all_gather.47, f32[128]{0:T(128)S(1)} %multiply_subtract_fusion.2, f32[8192,32]{0,1:T(8,128)S(1)} %get-tuple-element.27, f32[8192,1]{0,1:T(1,128)S(1)} %broadcast_in_dim.10, f32[8192,1]{0,1:T(1,128)S(1)} %bitcast.94), kind=kOutput, calls=%fused_computation | convolution fusion | flops 431521792 | bytes 5359104 | tf_op jit(solution)/shard_map/dot_general | solution.py:67
  246.1 0.2 fusion.30
  246.3 57.6 %psum.15 = f32[34,34]{1,0:T(8,128)S(1)} all-reduce(f32[34,34]{1,0:T(8,128)S(1)} %fusion.30), channel_id=1, replica_groups=mesh['pairs'=2,'src'=8,'tgt'=2] {'src','tgt'}, use_global_device_ids=true, to_apply=%region_15.0 | all-reduce | flops 1156 | bytes 9248 | tf_op jit(solution)/shard_map/psum | solution.py:69
  303.9 0.6 broadcast_multiply_fusion.1
  304.5 0.6 copy.16
  (11 shorter events, 0.2 us)
Async XLA Ops:
  7.2 3.0 copy-start
  7.2 47.8 %copy-start.3 = (f32[8192]{0:T(1024)S(1)}, f32[8192]{0:T(1024)}, u32[]{:S(2)}) copy-start(f32[8192]{0:T(1024)} %param.6) | copy-start | bytes 98308
  7.2 46.0 %all-gather.11.cloned.1.call-start = ((), (), s32[]{:S(2)}) async-start(), calls=%async_computation.4 | async-start | bytes 1179648 | tf_op jit(solution)/shard_map/all_gather | solution.py:36
  58.8 5.8 %copy-start.2 = (f32[128,8192]{1,0:T(8,128)}, f32[128,8192]{1,0:T(8,128)S(1)}, u32[]{:S(2)}) copy-start(f32[128,8192]{1,0:T(8,128)S(1)} %get-tuple-element.38) | copy-start | bytes 12582916
  64.5 10.0 %all-to-all-start = ((f32[1,8,1024]{2,0,1:T(1,128)}), f32[1,8,1024]{2,0,1:T(1,128)S(1)}, u32[]{:S(2)}, u32[]{:S(2)}) async-start(f32[1,8,1024]{2,0,1:T(1,128)} %bitcast.11), calls=%async_computation | async-start | bytes 65536 | tf_op jit(solution)/shard_map/all_to_all | solution.py:59
  74.6 10.0 %all-to-all-start.1 = ((f32[1,8,1024]{2,0,1:T(1,128)}), f32[1,8,1024]{2,0,1:T(1,128)S(1)}, u32[]{:S(2)}, u32[]{:S(2)}) async-start(f32[1,8,1024]{2,0,1:T(1,128)} %bitcast.12), calls=%async_computation.1 | async-start | bytes 65536 | tf_op jit(solution)/shard_map/all_to_all | solution.py:60
  183.5 5.8 %copy-start.1 = (f32[128,8192]{1,0:T(8,128)}, f32[128,8192]{1,0:T(8,128)S(1)}, u32[]{:S(2)}) copy-start(f32[128,8192]{1,0:T(8,128)S(1)} %get-tuple-element.40) | copy-start | bytes 12582916
  188.1 51.8 %copy-start.4 = (f32[128]{0:T(128)}, f32[128]{0:T(128)S(1)}, u32[]{:S(2)}) copy-start(f32[128]{0:T(128)S(1)} %multiply_subtract_fusion.2) | copy-start | bytes 1540
  189.3 10.0 %all-to-all-start.2 = ((f32[1,8,1024]{2,0,1:T(1,128)}), f32[1,8,1024]{2,0,1:T(1,128)S(1)}, u32[]{:S(2)}, u32[]{:S(2)}) async-start(f32[1,8,1024]{2,0,1:T(1,128)} %bitcast.19), calls=%async_computation.2 | async-start | bytes 65536 | tf_op jit(solution)/shard_map/all_to_all | solution.py:59
  199.3 10.0 %all-to-all-start.3 = ((f32[1,8,1024]{2,0,1:T(1,128)}), f32[1,8,1024]{2,0,1:T(1,128)S(1)}, u32[]{:S(2)}, u32[]{:S(2)}) async-start(f32[1,8,1024]{2,0,1:T(1,128)} %bitcast.20), calls=%async_computation.3 | async-start | bytes 65536 | tf_op jit(solution)/shard_map/all_to_all | solution.py:60
Sparse Core Ops, SparseCore 0:
  10.1 42.9 all-gather.10
where the time goes:
time: 313 us; the launch traced here: 312 us
  blocking collectives  186 us (59%)
  waiting for transfers between devices  62.4 us (20%)
  matrix products  21 us (7%)
  between operations  14.2 us (5%)
  starting transfers between devices  13.4 us (4%)
  other arithmetic  12.7 us (4%)
    psum x2, blocking collectives, shards(): core_matrix = -2.0 * lax.psum(core_part, ('src', 'tgt'))  115 us
    all_gather x2, blocking collectives, shards(): tgt_dual = lax.all_gather(dual_piece, 'src', axis=0, tiled=True)  61.2 us
    all_gather x1, waiting for transfers between devices, shards(): tgt_rows = lax.all_gather(tgt_feat, 'src', axis=1, tiled=True)  42.7 us
    all_to_all x2, waiting for transfers between devices, shards(): lax.all_to_all(col_total[None, :], 'src', split_axis=1, concat_axis=0, ti...  13.2 us
    dot_general x2, matrix products, shards(): weighted = jnp.dot(coupling, tgt_left, precision=HIGH)  12.4 us
    dot_general x2, matrix products, shards(): linear = jnp.dot(projected, tgt_right.T, precision=HIGH)  7.61 us
    reduce_sum x2, other arithmetic, shards(): col_total = jnp.sum(col_exp, axis=0)  7.45 us
    all_gather x4, blocking collectives, merged(): everything = jax.tree.map(lambda part: lax.all_gather(part, axis), array)  7.19 us
  transfers between devices with their start and end apart: 5, of which 5 were waited for; matrix products, arithmetic and copies ran while one was open for 3% of the time, Pallas kernels for 0%

commit v1 on v0

--- a/solution.py
+++ b/solution.py
@@ -66,7 +66,7 @@
         coupling = jnp.exp((src_dual[:, None] + tgt_dual[None, :] - linear) / EPSILON)
         weighted = jnp.dot(coupling, tgt_left, precision=HIGH)
         core_part = jnp.dot(src_right.T, weighted, precision=HIGH)
-        core_matrix = -2.0 * lax.psum(core_part, ("src", "tgt"))
+        core_matrix = -2.0 * jnp.sum(lax.all_gather(core_part, ("src", "tgt")), axis=0)
     return (src_dual, tgt_dual, core_matrix)
 
 

time: 313 us -> 235 us (0.75)
  blocking collectives: 186 us -> 108 us
    psum x2 -> x0, blocking collectives: 115 us -> none  [shards(): core_matrix = -2.0 * lax.psum(core_part, ('src', 'tgt'))]
    all_gather x0 -> x2, blocking collectives: none -> 37.4 us  [shards(): lax.all_gather(core_part, ('src', 'tgt'))]
where the time goes in v1:
time: 235 us; the launch traced here: 234 us
  blocking collectives  108 us (46%)
  waiting for transfers between devices  62.4 us (27%)
  matrix products  21 us (9%)
  between operations  14.2 us (6%)
  starting transfers between devices  13.4 us (6%)
  other arithmetic  12.8 us (5%)
    all_gather x2, blocking collectives, shards(): tgt_dual = lax.all_gather(dual_piece, 'src', axis=0, tiled=True)  61.2 us
    all_gather x1, waiting for transfers between devices, shards(): tgt_rows = lax.all_gather(tgt_feat, 'src', axis=1, tiled=True)  42.7 us
    all_gather x2, blocking collectives, shards(): lax.all_gather(core_part, ('src', 'tgt'))  37.4 us
    all_to_all x2, waiting for transfers between devices, shards(): lax.all_to_all(col_total[None, :], 'src', split_axis=1, concat_axis=0, ti...  13.2 us
    dot_general x2, matrix products, shards(): weighted = jnp.dot(coupling, tgt_left, precision=HIGH)  12.4 us
    dot_general x2, matrix products, shards(): linear = jnp.dot(projected, tgt_right.T, precision=HIGH)  7.61 us
    reduce_sum x2, other arithmetic, shards(): col_total = jnp.sum(col_exp, axis=0)  7.45 us
    all_gather x4, blocking collectives, merged(): everything = jax.tree.map(lambda part: lax.all_gather(part, axis), array)  7.19 us
  transfers between devices with their start and end apart: 5, of which 5 were waited for; matrix products, arithmetic and copies ran while one was open for 3% of the time, Pallas kernels for 0%

profile of v1, /device:TPU:0, one launch (start us, length us, event | category | flops | bytes accessed | tf_op | source)
XLA Modules:
  0.0 234.1 jit_solution(6377584103374106465)
XLA Ops:
  7.2 0.0 copy-start
  7.2 0.0 copy-start.3
  7.2 0.0 all-gather.15.cloned.1.call-start
  7.2 0.7 all-gather.15.cloned.1.call-update
  7.9 2.2 all_gather.48
  10.1 0.0 copy-done
  10.1 0.3 fusion.30
  10.4 42.7 %all-gather.15.cloned.1.call-done = f32[8,4,8192]{2,1,0:T(4,128)} async-done(((f32[1,4,8192]{2,1,0:T(4,128)}), f32[8,4,8192]{2,1,0:T(4,128)}) %all-gather.15.cloned.1.call-update) | async-done | bytes 1048592 | tf_op jit(solution)/shard_map/all_gather | solution.py:36
  53.2 1.6 reshape.134
  54.8 0.2 broadcast_multiply_fusion
  55.0 0.0 copy-done.3
  55.0 3.8 %fusion.10 = (f32[128]{0:T(128)S(1)}, f32[128,8192]{1,0:T(8,128)S(1)}) fusion(f32[8192]{0:T(1024)S(1)} %copy-done.3, f32[128,34]{1,0:T(8,128)S(1)} %fusion.30, f32[8192,32]{0,1:T(8,128)S(1)} %bitcast.93, f32[8192,1]{0,1:T(1,128)S(1)} %bitcast.95, f32[8192,1]{0,1:T(1,128)S(1)} %broadcast_in_dim.10), kind=kOutput, calls=%fused_computation.18 | convolution fusion | flops 431521664 | bytes 5359104 | tf_op jit(solution)/shard_map/dot_general | solution.py:48
  58.8 0.0 copy-start.2
  58.8 1.0 exponential_reduce_fusion.3
  59.8 1.8 all-gather.8
  61.6 1.8 all-gather.7
  63.4 1.2 fusion.11
  64.5 0.0 copy-done.2
  64.5 3.3 %all-to-all-start = ((f32[1,8,1024]{2,0,1:T(1,128)}), f32[1,8,1024]{2,0,1:T(1,128)S(1)}, u32[]{:S(2)}, u32[]{:S(2)}) async-start(f32[1,8,1024]{2,0,1:T(1,128)} %bitcast.11), calls=%async_computation | async-start | bytes 65536 | tf_op jit(solution)/shard_map/all_to_all | solution.py:59
  67.9 3.7 %exponential_reduce_fusion.2 = f32[8192]{0:T(1024)} fusion(f32[128,8192]{1,0:T(8,128)} %copy-done.2, f32[8192]{0:T(1024)} %fusion.11, f32[128]{0:T(128)S(1)} %multiply_subtract_fusion.3), kind=kLoop, calls=%fused_computation.14 | loop fusion | flops 4186112 | bytes 4260352 | tf_op jit(solution)/shard_map/reduce_sum | solution.py:57
  71.6 2.9 %all-to-all-done = f32[1,8,1024]{2,0,1:T(1,128)S(1)} async-done(((f32[1,8,1024]{2,0,1:T(1,128)}), f32[1,8,1024]{2,0,1:T(1,128)S(1)}, u32[]{:S(2)}, u32[]{:S(2)}) %all-to-all-start) | async-done | bytes 32800 | tf_op jit(solution)/shard_map/all_to_all | solution.py:59
  74.6 3.3 %all-to-all-start.1 = ((f32[1,8,1024]{2,0,1:T(1,128)}), f32[1,8,1024]{2,0,1:T(1,128)S(1)}, u32[]{:S(2)}, u32[]{:S(2)}) async-start(f32[1,8,1024]{2,0,1:T(1,128)} %bitcast.12), calls=%async_computation.1 | async-start | bytes 65536 | tf_op jit(solution)/shard_map/all_to_all | solution.py:60
  77.9 6.6 %all-to-all-done.1 = f32[1,8,1024]{2,0,1:T(1,128)S(1)} async-done(((f32[1,8,1024]{2,0,1:T(1,128)}), f32[1,8,1024]{2,0,1:T(1,128)S(1)}, u32[]{:S(2)}, u32[]{:S(2)}) %all-to-all-start.1) | async-done | bytes 32800 | tf_op jit(solution)/shard_map/all_to_all | solution.py:60
  84.6 30.6 %all_gather.54 = f32[8192]{0:T(1024)S(1)} all-gather(f32[1024]{0:T(1024)S(1)} %multiply_subtract_fusion.1), channel_id=1, replica_groups=mesh['pairs'=2,'src'=8,'tgt'=2] {'src'}, dimensions={0}, use_global_device_ids=true | all-gather | bytes 36864 | tf_op jit(solution)/shard_map/all_gather | solution.py:65
  115.2 6.2 %fusion.5 = f32[128,34]{1,0:T(8,128)S(1)} fusion(f32[128,8192]{1,0:T(8,128)} %copy-done.2, f32[8192]{0:T(1024)S(1)} %all_gather.54, f32[128]{0:T(128)S(1)} %multiply_subtract_fusion.3, f32[8192,32]{0,1:T(8,128)S(1)} %get-tuple-element.27, f32[8192,1]{0,1:T(1,128)S(1)} %broadcast_in_dim.10, f32[8192,1]{0,1:T(1,128)S(1)} %bitcast.96), kind=kOutput, calls=%fused_computation.9 | convolution fusion | flops 431521792 | bytes 5359104 | tf_op jit(solution)/shard_map/dot_general | solution.py:67
  121.4 0.2 convolution_bitcast_fusion.1
  121.6 18.8 %all-gather.9 = f32[16,34,34]{2,1,0:T(8,128)S(1)} all-gather(f32[1,34,34]{2,1,0:T(8,128)S(1)} %convolution_bitcast_fusion.1), channel_id=4, replica_groups=mesh['pairs'=2,'src'=8,'tgt'=2] {'src','tgt'}, dimensions={0}, use_global_device_ids=true | all-gather | bytes 78608 | tf_op jit(solution)/shard_map/all_gather | solution.py:69
  140.4 0.3 fusion.28
  140.7 3.8 %fusion.12 = (f32[128]{0:T(128)S(1)}, f32[128,8192]{1,0:T(8,128)S(1)}) fusion(f32[8192]{0:T(1024)S(1)} %all_gather.54, f32[128,34]{1,0:T(8,128)S(1)} %fusion.28, f32[8192,32]{0,1:T(8,128)S(1)} %bitcast.94, f32[8192,1]{0,1:T(1,128)S(1)} %bitcast.97, f32[8192,1]{0,1:T(1,128)S(1)} %broadcast_in_dim.10), kind=kOutput, calls=%fused_computation.20 | convolution fusion | flops 431521664 | bytes 5359104 | tf_op jit(solution)/shard_map/dot_general | solution.py:48
  144.5 0.0 copy-start.1
  144.6 1.0 exponential_reduce_fusion.1
  145.6 1.8 all-gather.11
  147.4 1.8 all-gather.10
  149.2 0.0 copy-start.4
  149.2 1.1 fusion.13
  150.3 0.0 copy-done.1
  150.3 3.3 %all-to-all-start.2 = ((f32[1,8,1024]{2,0,1:T(1,128)}), f32[1,8,1024]{2,0,1:T(1,128)S(1)}, u32[]{:S(2)}, u32[]{:S(2)}) async-start(f32[1,8,1024]{2,0,1:T(1,128)} %bitcast.20), calls=%async_computation.2 | async-start | bytes 65536 | tf_op jit(solution)/shard_map/all_to_all | solution.py:59
  153.7 3.7 %exponential_reduce_fusion = f32[8192]{0:T(1024)} fusion(f32[128,8192]{1,0:T(8,128)} %copy-done.1, f32[8192]{0:T(1024)} %fusion.13, f32[128]{0:T(128)S(1)} %multiply_subtract_fusion.2), kind=kLoop, calls=%fused_computation.5 | loop fusion | flops 4186112 | bytes 4260352 | tf_op jit(solution)/shard_map/reduce_sum | solution.py:57
  157.4 2.9 %all-to-all-done.2 = f32[1,8,1024]{2,0,1:T(1,128)S(1)} async-done(((f32[1,8,1024]{2,0,1:T(1,128)}), f32[1,8,1024]{2,0,1:T(1,128)S(1)}, u32[]{:S(2)}, u32[]{:S(2)}) %all-to-all-start.2) | async-done | bytes 32800 | tf_op jit(solution)/shard_map/all_to_all | solution.py:59
  160.3 3.3 %all-to-all-start.3 = ((f32[1,8,1024]{2,0,1:T(1,128)}), f32[1,8,1024]{2,0,1:T(1,128)S(1)}, u32[]{:S(2)}, u32[]{:S(2)}) async-start(f32[1,8,1024]{2,0,1:T(1,128)} %bitcast.21), calls=%async_computation.3 | async-start | bytes 65536 | tf_op jit(solution)/shard_map/all_to_all | solution.py:60
  163.7 6.6 %all-to-all-done.3 = f32[1,8,1024]{2,0,1:T(1,128)S(1)} async-done(((f32[1,8,1024]{2,0,1:T(1,128)}), f32[1,8,1024]{2,0,1:T(1,128)S(1)}, u32[]{:S(2)}, u32[]{:S(2)}) %all-to-all-start.3) | async-done | bytes 32800 | tf_op jit(solution)/shard_map/all_to_all | solution.py:60
  170.3 30.6 %all_gather.61 = f32[8192]{0:T(1024)S(1)} all-gather(f32[1024]{0:T(1024)S(1)} %multiply_subtract_fusion), channel_id=1, replica_groups=mesh['pairs'=2,'src'=8,'tgt'=2] {'src'}, dimensions={0}, use_global_device_ids=true | all-gather | bytes 36864 | tf_op jit(solution)/shard_map/all_gather | solution.py:65
  200.9 0.0 copy-done.4
  200.9 6.2 %fusion = f32[128,34]{1,0:T(8,128)S(1)} fusion(f32[128,8192]{1,0:T(8,128)} %copy-done.1, f32[8192]{0:T(1024)S(1)} %all_gather.61, f32[128]{0:T(128)S(1)} %multiply_subtract_fusion.2, f32[8192,32]{0,1:T(8,128)S(1)} %get-tuple-element.27, f32[8192,1]{0,1:T(1,128)S(1)} %broadcast_in_dim.10, f32[8192,1]{0,1:T(1,128)S(1)} %bitcast.98), kind=kOutput, calls=%fused_computation | convolution fusion | flops 431521792 | bytes 5359104 | tf_op jit(solution)/shard_map/dot_general | solution.py:67
  207.1 0.2 convolution_bitcast_fusion
  207.3 18.6 %all-gather.12 = f32[16,34,34]{2,1,0:T(8,128)S(1)} all-gather(f32[1,34,34]{2,1,0:T(8,128)S(1)} %convolution_bitcast_fusion), channel_id=7, replica_groups=mesh['pairs'=2,'src'=8,'tgt'=2] {'src','tgt'}, dimensions={0}, use_global_device_ids=true | all-gather | bytes 78608 | tf_op jit(solution)/shard_map/all_gather | solution.py:69
  226.0 0.6 broadcast_multiply_fusion.1
  226.6 0.6 copy.16
  (13 shorter events, 0.3 us)
Async XLA Ops:
  7.2 3.0 %copy-start = (f32[34,34]{1,0:T(8,128)S(1)}, f32[34,34]{1,0:T(8,128)}, u32[]{:S(2)}) copy-start(f32[34,34]{1,0:T(8,128)} %param.7) | copy-start | bytes 13876
  7.2 47.8 %copy-start.3 = (f32[8192]{0:T(1024)S(1)}, f32[8192]{0:T(1024)}, u32[]{:S(2)}) copy-start(f32[8192]{0:T(1024)} %param.6) | copy-start | bytes 98308
  7.2 46.0 %all-gather.15.cloned.1.call-start = ((), (), s32[]{:S(2)}) async-start(), calls=%async_computation.4 | async-start | bytes 1179648 | tf_op jit(solution)/shard_map/all_gather | solution.py:36
  58.8 5.8 %copy-start.2 = (f32[128,8192]{1,0:T(8,128)}, f32[128,8192]{1,0:T(8,128)S(1)}, u32[]{:S(2)}) copy-start(f32[128,8192]{1,0:T(8,128)S(1)} %get-tuple-element.38) | copy-start | bytes 12582916
  64.5 10.0 %all-to-all-start = ((f32[1,8,1024]{2,0,1:T(1,128)}), f32[1,8,1024]{2,0,1:T(1,128)S(1)}, u32[]{:S(2)}, u32[]{:S(2)}) async-start(f32[1,8,1024]{2,0,1:T(1,128)} %bitcast.11), calls=%async_computation | async-start | bytes 65536 | tf_op jit(solution)/shard_map/all_to_all | solution.py:59
  74.6 10.0 %all-to-all-start.1 = ((f32[1,8,1024]{2,0,1:T(1,128)}), f32[1,8,1024]{2,0,1:T(1,128)S(1)}, u32[]{:S(2)}, u32[]{:S(2)}) async-start(f32[1,8,1024]{2,0,1:T(1,128)} %bitcast.12), calls=%async_computation.1 | async-start | bytes 65536 | tf_op jit(solution)/shard_map/all_to_all | solution.py:60
  144.5 5.8 %copy-start.1 = (f32[128,8192]{1,0:T(8,128)}, f32[128,8192]{1,0:T(8,128)S(1)}, u32[]{:S(2)}) copy-start(f32[128,8192]{1,0:T(8,128)S(1)} %get-tuple-element.40) | copy-start | bytes 12582916
  149.2 51.8 %copy-start.4 = (f32[128]{0:T(128)}, f32[128]{0:T(128)S(1)}, u32[]{:S(2)}) copy-start(f32[128]{0:T(128)S(1)} %multiply_subtract_fusion.2) | copy-start | bytes 1540
  150.3 10.0 %all-to-all-start.2 = ((f32[1,8,1024]{2,0,1:T(1,128)}), f32[1,8,1024]{2,0,1:T(1,128)S(1)}, u32[]{:S(2)}, u32[]{:S(2)}) async-start(f32[1,8,1024]{2,0,1:T(1,128)} %bitcast.20), calls=%async_computation.2 | async-start | bytes 65536 | tf_op jit(solution)/shard_map/all_to_all | solution.py:59
  160.3 10.0 %all-to-all-start.3 = ((f32[1,8,1024]{2,0,1:T(1,128)}), f32[1,8,1024]{2,0,1:T(1,128)S(1)}, u32[]{:S(2)}, u32[]{:S(2)}) async-start(f32[1,8,1024]{2,0,1:T(1,128)} %bitcast.21), calls=%async_computation.3 | async-start | bytes 65536 | tf_op jit(solution)/shard_map/all_to_all | solution.py:60
Sparse Core Ops, SparseCore 0:
  10.1 42.9 all-gather.14
